TPU v7x, 128 devices: a whole 4x4x4 slice. The times are simulated.
128 devices in a mesh: leaf: 8 (over x, core), front: 16 (over z, y).
Axes of the slice: x: 4, y: 4, z: 4, core: 2. Of those that a mesh axis runs over, the one named last changes fastest.
Arguments:
- front_matrix: float32 [8, 2048, 2048], P('leaf', 'front'), as said below
- child_blocks: float32 [128, 8, 3, 128, 128], P(('leaf', 'front')), may hold values from -0.046875 to 0.046875
- child_target: int32 [128, 8, 3], P(('leaf', 'front')), may hold values from 0 to 15, as said below
- child_count: int32 [128, 8], P(('leaf', 'front')), may hold values from 1 to 3, as said below
- shot_rhs: float32 [8, 64, 2048], P('leaf'), may hold values from -6 to 6
Outputs:
- factored: float32 [8, 2048, 2048], P('leaf', 'front')
- eliminated: float32 [8, 64, 2048], P('leaf')
Inputs may be any that keep to these rules, and one draw needn't show every extreme that they name: `child_target`: A bucket's code places its block on a row block that the receiving device (leaf index of the bucket, front index of the sender) holds, at a column block no later than that row block. Slots from child_count on are empty and hold no data. In every draw some leaf index receives 3 live blocks from every sender. `front_matrix`: after the child blocks are added, the symmetric matrix that each front's lower triangle defines is positive definite.
All inputs are finite; a program needn't handle non-finite values.
Results may differ from a plain program's by a relative error of at most 0.00013.
Values sent between devices are 32-bit elements; how exact they have to be, the bound alone decides.
No kernel may reach another device: no remote copies, remote signals or barrier semaphores. Data moves between devices by JAX's collectives and lax.ppermute only.
A program may use at most 64 MiB of HBM per device.

v0:
```python
import jax
import jax.numpy as jnp
from jax import lax
from jax.sharding import PartitionSpec as P

BLOCK = 128
PIVOTS = 1024


def spread(value, axis, source):
    kept = jnp.where(lax.axis_index(axis) == source, value, 0).astype(value.dtype)
    return lax.psum(kept, axis)


def lower_sym(square):
    return jnp.tril(square) + jnp.swapaxes(jnp.tril(square, -1), -1, -2)


def right_solve(factor, values):
    solved = jax.scipy.linalg.solve_triangular(factor, jnp.swapaxes(values, 1, 2), lower=True)
    return jnp.swapaxes(solved, 1, 2)


def local(front_matrix, child_blocks, child_target, child_count, shot_rhs):
    fronts_here, rows_local, order_here = front_matrix.shape
    leaf_count = lax.axis_size("leaf")
    capacity = child_blocks.shape[2]
    slot_ids = lax.broadcasted_iota(jnp.int32, child_target.shape, 2)
    live_code = jnp.where(slot_ids < child_count[:, :, None], child_target, -1)
    arrived, codes = (
        lax.all_to_all(child_blocks, "leaf", split_axis=1, concat_axis=1, tiled=True),
        lax.all_to_all(live_code, "leaf", split_axis=1, concat_axis=1, tiled=True),
    )
    count_in = leaf_count * capacity
    flat_blocks = arrived.reshape(count_in, BLOCK * BLOCK)
    flat_codes = codes.reshape(count_in)
    block_cols = order_here // BLOCK
    block_rows = rows_local // BLOCK
    slot_total = fronts_here * block_rows * block_cols
    one_hot = (
        lax.broadcasted_iota(jnp.int32, (slot_total, count_in), 0) == flat_codes[None, :]
    ).astype(jnp.float32)
    summed = jnp.dot(
        one_hot, flat_blocks, precision=lax.Precision.HIGHEST, preferred_element_type=jnp.float32
    )
    extended = summed.reshape(fronts_here, block_rows, block_cols, BLOCK, BLOCK)
    extended = extended.transpose(0, 1, 3, 2, 4).reshape(fronts_here, rows_local, order_here)
    matrix = front_matrix + extended
    my_index = lax.axis_index("front")
    row_global = my_index * rows_local + lax.broadcasted_iota(jnp.int32, (rows_local, 1), 0)
    current_rhs = shot_rhs
    left_parts = []
    diag_parts = []
    solved_parts = []
    for pivot_step in range(PIVOTS // BLOCK):
        start_col = pivot_step * BLOCK
        end_col = start_col + BLOCK
        column_panel = matrix[:, :, start_col:end_col]
        owner_index = start_col // rows_local
        owner_offset = start_col - owner_index * rows_local
        identity_mat = jnp.broadcast_to(jnp.eye(BLOCK, dtype=jnp.float32), column_panel.shape)
        safe_square = jnp.where(my_index == owner_index, lower_sym(column_panel), identity_mat)
        own_factor = jnp.linalg.cholesky(safe_square)
        pivot_factor = spread(own_factor, "front", owner_index)
        my_panel = right_solve(pivot_factor, column_panel)
        my_panel = jnp.where(row_global < start_col, jnp.float32(0.0), my_panel)
        placed = jnp.where(my_index == owner_index, pivot_factor, my_panel)
        my_panel = my_panel.at[:, owner_offset : owner_offset + BLOCK].set(placed)
        full_panel = lax.all_gather(my_panel, "front", axis=1, tiled=True)
        tail_panel = full_panel[:, end_col:]
        update = jnp.einsum(
            "frb,fcb->frc",
            my_panel,
            tail_panel,
            precision=lax.Precision.HIGHEST,
            preferred_element_type=jnp.float32,
        )
        matrix = matrix.at[:, :, end_col:].add(-update)
        zeta = right_solve(pivot_factor, current_rhs[:, :, start_col:end_col])
        rhs_update = jnp.einsum(
            "fnb,fcb->fnc",
            zeta,
            tail_panel,
            precision=lax.Precision.HIGHEST,
            preferred_element_type=jnp.float32,
        )
        current_rhs = current_rhs.at[:, :, end_col:].add(-rhs_update)
        pivots_now = jnp.diagonal(pivot_factor, axis1=1, axis2=2)
        left_parts.append(my_panel / pivots_now[:, None, :])
        diag_parts.append(pivots_now * pivots_now)
        solved_parts.append(zeta * pivots_now[:, None, :])
    col_global = lax.broadcasted_iota(jnp.int32, (1, order_here), 1)
    combined = jnp.concatenate(left_parts + [matrix[:, :, PIVOTS:]], axis=2)
    combined = jnp.where(row_global < col_global, jnp.float32(0.0), combined)
    diag_full = jnp.concatenate(
        diag_parts + [jnp.zeros((fronts_here, order_here - PIVOTS), jnp.float32)], axis=1
    )
    on_diagonal = (row_global == col_global) & (col_global < PIVOTS)
    factored = jnp.where(on_diagonal, diag_full[:, None, :], combined)
    eliminated = jnp.concatenate(solved_parts + [current_rhs[:, :, PIVOTS:]], axis=2)
    return (factored, eliminated)


def solution(mesh):
    return jax.shard_map(
        local,
        mesh=mesh,
        in_specs=(
            P("leaf", "front", None),
            P(("leaf", "front"), None, None, None, None),
            P(("leaf", "front"), None, None),
            P(("leaf", "front"), None),
            P("leaf", None, None),
        ),
        out_specs=(P("leaf", "front", None), P("leaf", None, None)),
        check_vma=False,
    )
```

profile of v0, /device:TPU:0, one launch (start us, length us, event | category | flops | bytes accessed | tf_op | source)
XLA Modules:
  0.0 1286.4 jit_solution(12583845993747838078)
XLA Ops:
  8.6 9.4 all_to_all.10
  18.1 3.6 all-to-all-start.1
  24.9 18.3 %all-to-all-done.1 = f32[1,8,3,128,128]{4,3,2,0,1:T(8,128)S(1)} async-done(((f32[1,8,3,128,128]{4,3,2,0,1:T(8,128)}), f32[1,8,3,128,128]{4,3,2,0,1:T(8,128)S(1)}, u32[]{:S(2)}, u32[]{:S(2)}) %all-to-all-start.1) | async-done | bytes 1572896 | tf_op jit(solution)/shard_map/all_to_all | solution.py:31
  43.2 2.6 fusion.31
  45.8 2.6 copy.268
  50.1 11.7 custom-call.46
  63.9 81.6 %all-reduce.9.cloned.1.call-done = f32[1,128,128]{2,1,0:T(8,128)} async-done(((f32[1,128,128]{2,1,0:T(8,128)}), f32[1,128,128]{2,1,0:T(8,128)}) %all-reduce.9.cloned.1.call-update) | async-done | bytes 65552 | tf_op jit(solution)/shard_map/psum | solution.py:12
  146.3 9.8 custom-call.47
  160.2 41.1 %all-gather.9.cloned.1.call-done = f32[1,2048,128]{2,1,0:T(8,128)} async-done(((f32[1,128,128]{2,1,0:T(8,128)}), f32[1,2048,128]{2,1,0:T(8,128)}) %all-gather.9.cloned.1.call-update) | async-done | bytes 1048592 | tf_op jit(solution)/shard_map/all_gather | solution.py:69
  201.3 2.2 fusion.13
  203.9 11.7 custom-call.48
  217.7 80.3 %all-reduce.11.cloned.1.call-done = f32[1,128,128]{2,1,0:T(8,128)} async-done(((f32[1,128,128]{2,1,0:T(8,128)}), f32[1,128,128]{2,1,0:T(8,128)}) %all-reduce.11.cloned.1.call-update) | async-done | bytes 65552 | tf_op jit(solution)/shard_map/psum | solution.py:12
  298.8 9.8 custom-call.49
  312.1 41.7 %all-gather.11.cloned.1.call-done = f32[1,2048,128]{2,1,0:T(8,128)} async-done(((f32[1,128,128]{2,1,0:T(8,128)}), f32[1,2048,128]{2,1,0:T(8,128)}) %all-gather.11.cloned.1.call-update) | async-done | bytes 1048592 | tf_op jit(solution)/shard_map/all_gather | solution.py:69
  353.8 2.1 fusion.12
  356.3 11.7 custom-call.50
  370.1 80.3 %all-reduce.13.cloned.1.call-done = f32[1,128,128]{2,1,0:T(8,128)} async-done(((f32[1,128,128]{2,1,0:T(8,128)}), f32[1,128,128]{2,1,0:T(8,128)}) %all-reduce.13.cloned.1.call-update) | async-done | bytes 65552 | tf_op jit(solution)/shard_map/psum | solution.py:12
  451.2 9.8 custom-call.51
  461.1 2.0 gather_fusion.2
  465.9 40.3 %all-gather.13.cloned.1.call-done = f32[1,2048,128]{2,1,0:T(8,128)} async-done(((f32[1,128,128]{2,1,0:T(8,128)}), f32[1,2048,128]{2,1,0:T(8,128)}) %all-gather.13.cloned.1.call-update) | async-done | bytes 1048592 | tf_op jit(solution)/shard_map/all_gather | solution.py:69
  506.3 2.0 fusion.11
  508.6 11.7 custom-call.52
  523.3 79.7 %all-reduce.15.cloned.1.call-done = f32[1,128,128]{1,2,0:T(8,128)} async-done(((f32[1,128,128]{1,2,0:T(8,128)}), f32[1,128,128]{1,2,0:T(8,128)}) %all-reduce.15.cloned.1.call-update) | async-done | bytes 65552 | tf_op jit(solution)/shard_map/psum | solution.py:12
  603.9 9.8 custom-call.53
  613.7 2.0 gather_fusion.3
  617.3 42.3 %all-gather.15.cloned.1.call-done = f32[1,2048,128]{1,2,0:T(8,128)} async-done(((f32[1,128,128]{1,2,0:T(8,128)}), f32[1,2048,128]{1,2,0:T(8,128)}) %all-gather.15.cloned.1.call-update) | async-done | bytes 1048592 | tf_op jit(solution)/shard_map/all_gather | solution.py:69
  659.6 2.0 fusion.7
  661.9 11.7 custom-call.54
  675.9 80.3 %all-reduce.17.cloned.1.call-done = f32[1,128,128]{1,2,0:T(8,128)} async-done(((f32[1,128,128]{1,2,0:T(8,128)}), f32[1,128,128]{1,2,0:T(8,128)}) %all-reduce.17.cloned.1.call-update) | async-done | bytes 65552 | tf_op jit(solution)/shard_map/psum | solution.py:12
  757.1 9.8 custom-call.55
  766.9 2.0 gather_fusion.4
  770.2 42.6 %all-gather.17.cloned.1.call-done = f32[1,2048,128]{1,2,0:T(8,128)} async-done(((f32[1,128,128]{1,2,0:T(8,128)}), f32[1,2048,128]{1,2,0:T(8,128)}) %all-gather.17.cloned.1.call-update) | async-done | bytes 1048592 | tf_op jit(solution)/shard_map/all_gather | solution.py:69
  815.1 11.7 custom-call.56
  829.0 80.3 %all-reduce.19.cloned.1.call-done = f32[1,128,128]{1,2,0:T(8,128)} async-done(((f32[1,128,128]{1,2,0:T(8,128)}), f32[1,128,128]{1,2,0:T(8,128)}) %all-reduce.19.cloned.1.call-update) | async-done | bytes 65552 | tf_op jit(solution)/shard_map/psum | solution.py:12
  910.2 9.8 custom-call.57
  920.1 2.0 gather_fusion.5
  928.8 37.1 %all-gather.19.cloned.1.call-done = f32[1,2048,128]{1,2,0:T(8,128)} async-done(((f32[1,128,128]{1,2,0:T(8,128)}), f32[1,2048,128]{1,2,0:T(8,128)}) %all-gather.19.cloned.1.call-update) | async-done | bytes 1048592 | tf_op jit(solution)/shard_map/all_gather | solution.py:69
  968.1 11.7 custom-call.58
  982.0 80.3 %all-reduce.21.cloned.1.call-done = f32[1,128,128]{1,2,0:T(8,128)} async-done(((f32[1,128,128]{1,2,0:T(8,128)}), f32[1,128,128]{1,2,0:T(8,128)}) %all-reduce.21.cloned.1.call-update) | async-done | bytes 65552 | tf_op jit(solution)/shard_map/psum | solution.py:12
  1063.3 9.8 custom-call.59
  1073.1 2.0 gather_fusion.6
  1082.5 37.1 %all-gather.21.cloned.1.call-done = f32[1,2048,128]{1,2,0:T(8,128)} async-done(((f32[1,128,128]{1,2,0:T(8,128)}), f32[1,2048,128]{1,2,0:T(8,128)}) %all-gather.21.cloned.1.call-update) | async-done | bytes 1048592 | tf_op jit(solution)/shard_map/all_gather | solution.py:69
  1119.6 2.2 fusion.1
  1122.2 11.7 custom-call.60
  1138.0 78.5 %all-reduce.23.cloned.1.call-done = f32[1,128,128]{2,1,0:T(8,128)} async-done(((f32[1,128,128]{2,1,0:T(8,128)}), f32[1,128,128]{2,1,0:T(8,128)}) %all-reduce.23.cloned.1.call-update) | async-done | bytes 65552 | tf_op jit(solution)/shard_map/psum | solution.py:12
  1217.4 9.8 custom-call.61
  1234.3 38.1 %all-gather.23.cloned.1.call-done = f32[1,2048,128]{2,1,0:T(8,128)} async-done(((f32[1,128,128]{2,1,0:T(8,128)}), f32[1,2048,128]{2,1,0:T(8,128)}) %all-gather.23.cloned.1.call-update) | async-done | bytes 1048592 | tf_op jit(solution)/shard_map/all_gather | solution.py:69
  1272.4 2.4 fusion.36
  (260 shorter events, 77.9 us)
Async XLA Ops:
  18.1 25.1 %all-to-all-start.1 = ((f32[1,8,3,128,128]{4,3,2,0,1:T(8,128)}), f32[1,8,3,128,128]{4,3,2,0,1:T(8,128)S(1)}, u32[]{:S(2)}, u32[]{:S(2)}) async-start(f32[1,8,3,128,128]{4,3,2,0,1:T(8,128)} %bitcast.595), calls=%async_computation.1 | async-start | bytes 3145728 | tf_op jit(solution)/shard_map/all_to_all | solution.py:31
  21.7 123.8 %all-reduce.9.cloned.1.call-start = ((), (), s32[]{:S(2)}) async-start(), calls=%async_computation.2 | async-start | bytes 131072 | tf_op jit(solution)/shard_map/psum | solution.py:12
  63.8 137.5 %all-gather.9.cloned.1.call-start = ((), (), s32[]{:S(2)}) async-start(), calls=%async_computation.3 | async-start | bytes 1114112 | tf_op jit(solution)/shard_map/all_gather | solution.py:69
  159.9 138.1 %all-reduce.11.cloned.1.call-start = ((), (), s32[]{:S(2)}) async-start(), calls=%async_computation.4 | async-start | bytes 131072 | tf_op jit(solution)/shard_map/psum | solution.py:12
  217.6 136.2 %all-gather.11.cloned.1.call-start = ((), (), s32[]{:S(2)}) async-start(), calls=%async_computation.5 | async-start | bytes 1114112 | tf_op jit(solution)/shard_map/all_gather | solution.py:69
  311.5 138.8 %all-reduce.13.cloned.1.call-start = ((), (), s32[]{:S(2)}) async-start(), calls=%async_computation.6 | async-start | bytes 131072 | tf_op jit(solution)/shard_map/psum | solution.py:12
  370.0 136.2 %all-gather.13.cloned.1.call-start = ((), (), s32[]{:S(2)}) async-start(), calls=%async_computation.7 | async-start | bytes 1114112 | tf_op jit(solution)/shard_map/all_gather | solution.py:69
  461.0 47.3 %copy-start.16 = (f32[1,128,128]{1,2,0:T(8,128)}, f32[1,128,128]{1,2,0:T(8,128)S(1)}, u32[]{:S(2)}) copy-start(f32[1,128,128]{1,2,0:T(8,128)S(1)} %custom-call.51) | copy-start | bytes 196612
  464.0 139.0 %all-reduce.15.cloned.1.call-start = ((), (), s32[]{:S(2)}) async-start(), calls=%async_computation.8 | async-start | bytes 131072 | tf_op jit(solution)/shard_map/psum | solution.py:12
  522.6 137.0 %all-gather.15.cloned.1.call-start = ((), (), s32[]{:S(2)}) async-start(), calls=%async_computation.9 | async-start | bytes 1114112 | tf_op jit(solution)/shard_map/all_gather | solution.py:69
  613.7 3.6 copy-start.18
  616.7 139.5 %all-reduce.17.cloned.1.call-start = ((), (), s32[]{:S(2)}) async-start(), calls=%async_computation.10 | async-start | bytes 131072 | tf_op jit(solution)/shard_map/psum | solution.py:12
  616.9 42.6 %copy-start.14 = (f32[1,128,128]{1,2,0:T(8,128)S(1)}, f32[1,128,128]{1,2,0:T(8,128)}, u32[]{:S(2)}) copy-start(f32[1,128,128]{1,2,0:T(8,128)} %get-tuple-element.372) | copy-start | bytes 196612
  675.8 137.0 %all-gather.17.cloned.1.call-start = ((), (), s32[]{:S(2)}) async-start(), calls=%async_computation.11 | async-start | bytes 1114112 | tf_op jit(solution)/shard_map/all_gather | solution.py:69
  766.9 47.8 %copy-start.22 = (f32[1,128,128]{1,2,0:T(8,128)}, f32[1,128,128]{1,2,0:T(8,128)S(1)}, u32[]{:S(2)}) copy-start(f32[1,128,128]{1,2,0:T(8,128)S(1)} %custom-call.55) | copy-start | bytes 196612
  769.9 139.4 %all-reduce.19.cloned.1.call-start = ((), (), s32[]{:S(2)}) async-start(), calls=%async_computation.12 | async-start | bytes 131072 | tf_op jit(solution)/shard_map/psum | solution.py:12
  814.7 110.4 %copy-start.15 = (f32[1,64,2048]{2,1,0:T(8,128)S(1)}, f32[1,64,2048]{2,1,0:T(8,128)}, u32[]{:S(2)}) copy-start(f32[1,64,2048]{2,1,0:T(8,128)} %param.78) | copy-start | bytes 1572868
  814.7 111.2 %copy-start = (f32[1,2048,128]{2,1,0:T(8,128)S(1)}, f32[1,2048,128]{2,1,0:T(8,128)}, u32[]{:S(2)}) copy-start(f32[1,2048,128]{2,1,0:T(8,128)} %all-gather.9.cloned.1.call-done) | copy-start | bytes 3145732
  828.9 137.0 %all-gather.19.cloned.1.call-start = ((), (), s32[]{:S(2)}) async-start(), calls=%async_computation.13 | async-start | bytes 1114112 | tf_op jit(solution)/shard_map/all_gather | solution.py:69
  920.0 7.1 copy-start.20
  923.0 42.9 %copy-start.13 = (f32[1,128,128]{1,2,0:T(8,128)S(1)}, f32[1,128,128]{1,2,0:T(8,128)}, u32[]{:S(2)}) copy-start(f32[1,128,128]{1,2,0:T(8,128)} %get-tuple-element.376) | copy-start | bytes 196612
  923.0 139.3 %all-reduce.21.cloned.1.call-start = ((), (), s32[]{:S(2)}) async-start(), calls=%async_computation.14 | async-start | bytes 131072 | tf_op jit(solution)/shard_map/psum | solution.py:12
  967.7 109.2 %copy-start.1 = (f32[1,2048,128]{2,1,0:T(8,128)S(1)}, f32[1,2048,128]{2,1,0:T(8,128)}, u32[]{:S(2)}) copy-start(f32[1,2048,128]{2,1,0:T(8,128)} %all-gather.11.cloned.1.call-done) | copy-start | bytes 3145732
  967.7 109.2 %copy-start.6 = (f32[1,64,1920]{2,1,0:T(8,128)S(1)}, f32[1,64,1920]{2,1,0:T(8,128)}, u32[]{:S(2)}) copy-start(f32[1,64,1920]{2,1,0:T(8,128)} %copy-done.5) | copy-start | bytes 1474564
  982.0 96.1 %copy-start.17 = (f32[1,128,128]{1,2,0:T(8,128)S(1)}, f32[1,128,128]{1,2,0:T(8,128)}, u32[]{:S(2)}) copy-start(f32[1,128,128]{1,2,0:T(8,128)} %copy-done.16) | copy-start | bytes 196612
  982.0 137.6 %all-gather.21.cloned.1.call-start = ((), (), s32[]{:S(2)}) async-start(), calls=%async_computation.15 | async-start | bytes 1114112 | tf_op jit(solution)/shard_map/all_gather | solution.py:69
  1063.2 15.7 %copy-start.2 = (f32[1,2048,128]{2,1,0:T(8,128)S(1)}, f32[1,2048,128]{2,1,0:T(8,128)}, u32[]{:S(2)}) copy-start(f32[1,2048,128]{2,1,0:T(8,128)} %all-gather.13.cloned.1.call-done) | copy-start | bytes 3145732
  1073.1 3.8 copy-start.24
  1075.1 3.8 copy-start.26
  1076.7 139.9 %all-reduce.23.cloned.1.call-start = ((), (), s32[]{:S(2)}) async-start(), calls=%async_computation.16 | async-start | bytes 131072 | tf_op jit(solution)/shard_map/psum | solution.py:12
  1076.9 3.1 copy-start.19
  1076.9 3.9 copy-start.3
  1078.9 2.5 copy-start.23
  1081.4 0.9 copy-start.8
  1081.4 38.2 %copy-start.11 = (f32[1,128,128]{1,2,0:T(8,128)S(1)}, f32[1,128,128]{1,2,0:T(8,128)}, u32[]{:S(2)}) copy-start(f32[1,128,128]{1,2,0:T(8,128)} %get-tuple-element.378) | copy-start | bytes 196612
  1082.5 54.0 %copy-start.4 = (f32[1,2048,128]{1,2,0:T(8,128)S(1)}, f32[1,2048,128]{1,2,0:T(8,128)}, u32[]{:S(2)}) copy-start(f32[1,2048,128]{1,2,0:T(8,128)} %all-gather.17.cloned.1.call-done) | copy-start | bytes 3145732
  1122.0 107.2 %copy-start.30 = (pred[128]{0:T(512)(128)(4,1)S(1)}, pred[128]{0:T(512)(128)(4,1)}, u32[]{:S(2)}) copy-start(pred[128]{0:T(512)(128)(4,1)} %broadcast_compare_fusion) | copy-start | bytes 388
  1122.1 108.0 %copy-start.21 = (f32[1,128,128]{1,2,0:T(8,128)S(1)}, f32[1,128,128]{1,2,0:T(8,128)}, u32[]{:S(2)}) copy-start(f32[1,128,128]{1,2,0:T(8,128)} %copy-done.20) | copy-start | bytes 196612
  1134.0 97.0 %copy-start.7 = (f32[1,2048,128]{1,2,0:T(8,128)S(1)}, f32[1,2048,128]{1,2,0:T(8,128)}, u32[]{:S(2)}) copy-start(f32[1,2048,128]{1,2,0:T(8,128)} %all-gather.19.cloned.1.call-done) | copy-start | bytes 3145732
  1136.2 136.2 %all-gather.23.cloned.1.call-start = ((), (), s32[]{:S(2)}) async-start(), calls=%async_computation.17 | async-start | bytes 1114112 | tf_op jit(solution)/shard_map/all_gather | solution.py:69
  1138.0 93.4 %copy-start.27 = (f32[128]{0:T(128)S(1)}, f32[128]{0:T(128)}, u32[]{:S(2)}) copy-start(f32[128]{0:T(128)} %copy-done.26) | copy-start | bytes 1540
  1138.0 93.5 %copy-start.25 = (f32[1,128,128]{1,2,0:T(8,128)S(1)}, f32[1,128,128]{1,2,0:T(8,128)}, u32[]{:S(2)}) copy-start(f32[1,128,128]{1,2,0:T(8,128)} %copy-done.24) | copy-start | bytes 196612
  1138.0 94.3 %copy-start.9 = (f32[1,2048,128]{1,2,0:T(8,128)S(1)}, f32[1,2048,128]{1,2,0:T(8,128)}, u32[]{:S(2)}) copy-start(f32[1,2048,128]{1,2,0:T(8,128)} %all-gather.21.cloned.1.call-done) | copy-start | bytes 3145732
  1231.0 41.5 %copy-start.12 = (f32[1,128,128]{2,1,0:T(8,128)S(1)}, f32[1,128,128]{2,1,0:T(8,128)}, u32[]{:S(2)}) copy-start(f32[1,128,128]{2,1,0:T(8,128)} %get-tuple-element.380) | copy-start | bytes 196612
  1232.3 42.6 %copy-start.31 = (s32[128]{0:T(128)S(1)}, s32[128]{0:T(128)}, u32[]{:S(2)}) copy-start(s32[128]{0:T(128)} %iota_add_fusion.1) | copy-start | bytes 1540
  1276.6 1.3 copy-start.10
  1276.6 1.6 copy-start.28
  1278.9 0.8 copy-start.29
  (1 other events, 0.8 us)
Sparse Core Ops, SparseCore 0:
  63.9 81.5 all-reduce.8
  160.0 41.2 all-gather.8
  217.7 80.2 all-reduce.10
  311.7 42.1 all-gather.10
  370.1 80.1 all-reduce.12
  464.1 42.1 all-gather.12
  522.7 80.2 all-reduce.14
  616.8 42.7 all-gather.14
  675.9 80.2 all-reduce.16
  770.0 42.7 all-gather.16
  829.0 80.2 all-reduce.18
  923.1 42.7 all-gather.18
  982.1 80.1 all-reduce.20
  1076.8 42.7 all-gather.20
  1136.3 80.2 all-reduce.22
  1230.3 42.1 all-gather.22
where the time goes:
time: 1300 us; the launch traced here: 1290 us
  waiting for transfers between devices  980 us (75%)
  other arithmetic  202 us (16%)
  matrix products  41.7 us (3%)
  local copies, waits for them, and re-layouts  31.6 us (2%)
  between operations  15.4 us (1%)
    psum x8, waiting for transfers between devices, spread(): return lax.psum(kept, axis)  641 us
    all_gather x8, waiting for transfers between devices, local(): full_panel = lax.all_gather(my_panel, 'front', axis=1, tiled=True)  320 us
    another operation x24, other arithmetic, local(): own_factor = jnp.linalg.cholesky(safe_square)  99.8 us
    another operation x16, other arithmetic, right_solve(): jax.scipy.linalg.solve_triangular(factor, jnp.swapaxes(values, 1, 2), low...  85.3 us
  transfers between devices with their start and end apart: 17, of which 17 were waited for; matrix products, arithmetic and copies ran while one was open for 2% of the time, Pallas kernels for 0%

commit v1 on v0

--- a/solution.py
+++ b/solution.py
@@ -9,7 +9,11 @@
 
 def spread(value, axis, source):
     kept = jnp.where(lax.axis_index(axis) == source, value, 0).astype(value.dtype)
-    return lax.psum(kept, axis)
+
+    def number_space_now(local_values):
+        return jnp.sum(lax.all_gather(local_values, axis_name=axis), axis=0)
+
+    return number_space_now(kept)
 
 
 def lower_sym(square):

time: 1300 us -> 993 us (0.76)
  waiting for transfers between devices: 980 us -> 680 us
    psum x8 -> x0, waiting for transfers between devices: 641 us -> none  [spread(): return lax.psum(kept, axis)]
    all_gather x0 -> x8, waiting for transfers between devices: none -> 332 us  [number_space_now(): return jnp.sum(lax.all_gather(local_values, axis_name=axis), axis=0)]
where the time goes in v1:
time: 993 us; the launch traced here: 984 us
  waiting for transfers between devices  680 us (68%)
  other arithmetic  203 us (20%)
  matrix products  40.2 us (4%)
  local copies, waits for them, and re-layouts  30 us (3%)
  between operations  15.5 us (2%)
    all_gather x8, waiting for transfers between devices, number_space_now(): return jnp.sum(lax.all_gather(local_values, axis_name=axis), axis=0)  332 us
    all_gather x8, waiting for transfers between devices, local(): full_panel = lax.all_gather(my_panel, 'front', axis=1, tiled=True)  329 us
    another operation x24, other arithmetic, local(): own_factor = jnp.linalg.cholesky(safe_square)  99.6 us
    another operation x16, other arithmetic, right_solve(): jax.scipy.linalg.solve_triangular(factor, jnp.swapaxes(values, 1, 2), low...  80.7 us
  transfers between devices with their start and end apart: 17, of which 17 were waited for; matrix products, arithmetic and copies ran while one was open for 2% of the time, Pallas kernels for 0%

profile of v1, /device:TPU:0, one launch (start us, length us, event | category | flops | bytes accessed | tf_op | source)
XLA Modules:
  0.0 984.3 jit_solution(12024786861373492588)
XLA Ops:
  8.6 9.4 all_to_all.10
  18.1 3.6 all-to-all-start.1
  24.9 18.3 %all-to-all-done.1 = f32[1,8,3,128,128]{4,3,2,0,1:T(8,128)S(1)} async-done(((f32[1,8,3,128,128]{4,3,2,0,1:T(8,128)}), f32[1,8,3,128,128]{4,3,2,0,1:T(8,128)S(1)}, u32[]{:S(2)}, u32[]{:S(2)}) %all-to-all-start.1) | async-done | bytes 1572896 | tf_op jit(solution)/shard_map/all_to_all | solution.py:35
  43.2 2.6 fusion.31
  45.8 2.6 copy.467
  50.1 11.7 %custom-call.46 = f32[1,128,128]{2,1,0:T(8,128)S(1)} custom-call(f32[1,128,128]{2,1,0:T(8,128)S(1)} %copy.474), custom_call_target="Cholesky" | custom-call | tf_op jit(solution)/shard_map/jit(cholesky)/cholesky | solution.py:67
  63.9 43.5 %all-gather.41.cloned.1.call-done = f32[16,128,128]{2,1,0:T(8,128)} async-done(((f32[1,128,128]{2,1,0:T(8,128)}), f32[16,128,128]{2,1,0:T(8,128)}) %all-gather.41.cloned.1.call-update) | async-done | bytes 1048592 | tf_op jit(solution)/shard_map/all_gather | solution.py:14
  109.9 9.8 custom-call.47
  121.0 41.9 %all-gather.25.cloned.1.call-done = f32[1,2048,128]{2,1,0:T(8,128)} async-done(((f32[1,128,128]{2,1,0:T(8,128)}), f32[1,2048,128]{2,1,0:T(8,128)}) %all-gather.25.cloned.1.call-update) | async-done | bytes 1048592 | tf_op jit(solution)/shard_map/all_gather | solution.py:73
  162.9 2.2 fusion.13
  165.5 11.7 %custom-call.48 = f32[1,128,128]{2,1,0:T(8,128)S(1)} custom-call(f32[1,128,128]{2,1,0:T(8,128)S(1)} %copy.483), custom_call_target="Cholesky" | custom-call | tf_op jit(solution)/shard_map/jit(cholesky)/cholesky | solution.py:67
  179.3 42.2 %all-gather.43.cloned.1.call-done = f32[16,128,128]{2,1,0:T(8,128)} async-done(((f32[1,128,128]{2,1,0:T(8,128)}), f32[16,128,128]{2,1,0:T(8,128)}) %all-gather.43.cloned.1.call-update) | async-done | bytes 1048592 | tf_op jit(solution)/shard_map/all_gather | solution.py:14
  224.0 9.8 custom-call.49
  235.4 41.7 %all-gather.27.cloned.1.call-done = f32[1,2048,128]{2,1,0:T(8,128)} async-done(((f32[1,128,128]{2,1,0:T(8,128)}), f32[1,2048,128]{2,1,0:T(8,128)}) %all-gather.27.cloned.1.call-update) | async-done | bytes 1048592 | tf_op jit(solution)/shard_map/all_gather | solution.py:73
  277.1 2.1 fusion.12
  279.5 11.7 %custom-call.50 = f32[1,128,128]{2,1,0:T(8,128)S(1)} custom-call(f32[1,128,128]{2,1,0:T(8,128)S(1)} %copy.492), custom_call_target="Cholesky" | custom-call | tf_op jit(solution)/shard_map/jit(cholesky)/cholesky | solution.py:67
  293.3 42.2 %all-gather.45.cloned.1.call-done = f32[16,128,128]{2,1,0:T(8,128)} async-done(((f32[1,128,128]{2,1,0:T(8,128)}), f32[16,128,128]{2,1,0:T(8,128)}) %all-gather.45.cloned.1.call-update) | async-done | bytes 1048592 | tf_op jit(solution)/shard_map/all_gather | solution.py:14
  338.1 9.8 custom-call.51
  349.2 41.9 %all-gather.29.cloned.1.call-done = f32[1,2048,128]{2,1,0:T(8,128)} async-done(((f32[1,128,128]{2,1,0:T(8,128)}), f32[1,2048,128]{2,1,0:T(8,128)}) %all-gather.29.cloned.1.call-update) | async-done | bytes 1048592 | tf_op jit(solution)/shard_map/all_gather | solution.py:73
  391.1 2.0 fusion.11
  393.5 11.7 %custom-call.52 = f32[1,128,128]{2,1,0:T(8,128)S(1)} custom-call(f32[1,128,128]{2,1,0:T(8,128)S(1)} %fusion.97), custom_call_target="Cholesky" | custom-call | tf_op jit(solution)/shard_map/jit(cholesky)/cholesky | solution.py:67
  409.7 40.0 %all-gather.47.cloned.1.call-done = f32[16,128,128]{2,1,0:T(8,128)} async-done(((f32[1,128,128]{2,1,0:T(8,128)}), f32[16,128,128]{2,1,0:T(8,128)}) %all-gather.47.cloned.1.call-update) | async-done | bytes 1048592 | tf_op jit(solution)/shard_map/all_gather | solution.py:14
  452.5 9.8 custom-call.53
  463.9 42.2 %all-gather.31.cloned.1.call-done = f32[1,2048,128]{1,2,0:T(8,128)} async-done(((f32[1,128,128]{1,2,0:T(8,128)}), f32[1,2048,128]{1,2,0:T(8,128)}) %all-gather.31.cloned.1.call-update) | async-done | bytes 1048592 | tf_op jit(solution)/shard_map/all_gather | solution.py:73
  506.2 2.0 fusion.7
  508.5 11.7 %custom-call.54 = f32[1,128,128]{2,1,0:T(8,128)S(1)} custom-call(f32[1,128,128]{2,1,0:T(8,128)S(1)} %fusion.92), custom_call_target="Cholesky" | custom-call | tf_op jit(solution)/shard_map/jit(cholesky)/cholesky | solution.py:67
  522.5 42.2 %all-gather.49.cloned.1.call-done = f32[16,128,128]{2,1,0:T(8,128)} async-done(((f32[1,128,128]{2,1,0:T(8,128)}), f32[16,128,128]{2,1,0:T(8,128)}) %all-gather.49.cloned.1.call-update) | async-done | bytes 1048592 | tf_op jit(solution)/shard_map/all_gather | solution.py:14
  567.5 9.8 custom-call.55
  578.6 42.6 %all-gather.33.cloned.1.call-done = f32[1,2048,128]{1,2,0:T(8,128)} async-done(((f32[1,128,128]{1,2,0:T(8,128)}), f32[1,2048,128]{1,2,0:T(8,128)}) %all-gather.33.cloned.1.call-update) | async-done | bytes 1048592 | tf_op jit(solution)/shard_map/all_gather | solution.py:73
  621.2 1.9 fusion.5
  623.5 11.7 %custom-call.56 = f32[1,128,128]{2,1,0:T(8,128)S(1)} custom-call(f32[1,128,128]{2,1,0:T(8,128)S(1)} %fusion.87), custom_call_target="Cholesky" | custom-call | tf_op jit(solution)/shard_map/jit(cholesky)/cholesky | solution.py:67
  637.5 42.2 %all-gather.51.cloned.1.call-done = f32[16,128,128]{2,1,0:T(8,128)} async-done(((f32[1,128,128]{2,1,0:T(8,128)}), f32[16,128,128]{2,1,0:T(8,128)}) %all-gather.51.cloned.1.call-update) | async-done | bytes 1048592 | tf_op jit(solution)/shard_map/all_gather | solution.py:14
  682.5 9.8 custom-call.57
  693.8 42.4 %all-gather.35.cloned.1.call-done = f32[1,2048,128]{1,2,0:T(8,128)} async-done(((f32[1,128,128]{1,2,0:T(8,128)}), f32[1,2048,128]{1,2,0:T(8,128)}) %all-gather.35.cloned.1.call-update) | async-done | bytes 1048592 | tf_op jit(solution)/shard_map/all_gather | solution.py:73
  736.2 1.9 fusion.3
  738.4 11.7 %custom-call.58 = f32[1,128,128]{2,1,0:T(8,128)S(1)} custom-call(f32[1,128,128]{2,1,0:T(8,128)S(1)} %fusion.82), custom_call_target="Cholesky" | custom-call | tf_op jit(solution)/shard_map/jit(cholesky)/cholesky | solution.py:67
  752.4 42.2 %all-gather.53.cloned.1.call-done = f32[16,128,128]{2,1,0:T(8,128)} async-done(((f32[1,128,128]{2,1,0:T(8,128)}), f32[16,128,128]{2,1,0:T(8,128)}) %all-gather.53.cloned.1.call-update) | async-done | bytes 1048592 | tf_op jit(solution)/shard_map/all_gather | solution.py:14
  798.0 1.6 copy.535
  799.5 11.3 %custom-call.59 = f32[1,128,128]{1,2,0:T(8,128)} custom-call(f32[1,128,128]{2,1,0:T(8,128)} %copy.535), custom_call_target="InvertDiagBlocksLowerTriangular" | custom-call | tf_op jit(solution)/shard_map/jit(_solve_triangular)/triangular_solve | solution.py:24
  810.8 1.8 divide_dynamic-update-slice_fusion
  817.1 38.3 %all-gather.37.cloned.1.call-done = f32[1,2048,128]{1,2,0:T(8,128)} async-done(((f32[1,128,128]{1,2,0:T(8,128)}), f32[1,2048,128]{1,2,0:T(8,128)}) %all-gather.37.cloned.1.call-update) | async-done | bytes 1048592 | tf_op jit(solution)/shard_map/all_gather | solution.py:73
  855.5 2.2 fusion.1
  858.0 11.7 %custom-call.60 = f32[1,128,128]{2,1,0:T(8,128)S(1)} custom-call(f32[1,128,128]{2,1,0:T(8,128)S(1)} %fusion.77), custom_call_target="Cholesky" | custom-call | tf_op jit(solution)/shard_map/jit(cholesky)/cholesky | solution.py:67
  877.1 37.3 %all-gather.55.cloned.1.call-done = f32[16,128,128]{2,1,0:T(8,128)} async-done(((f32[1,128,128]{2,1,0:T(8,128)}), f32[16,128,128]{2,1,0:T(8,128)}) %all-gather.55.cloned.1.call-update) | async-done | bytes 1048592 | tf_op jit(solution)/shard_map/all_gather | solution.py:14
  915.8 9.8 custom-call.61
  932.0 38.2 %all-gather.39.cloned.1.call-done = f32[1,2048,128]{2,1,0:T(8,128)} async-done(((f32[1,128,128]{2,1,0:T(8,128)}), f32[1,2048,128]{2,1,0:T(8,128)}) %all-gather.39.cloned.1.call-update) | async-done | bytes 1048592 | tf_op jit(solution)/shard_map/all_gather | solution.py:73
  970.2 2.5 fusion.36
  972.7 1.7 select_select_fusion
  (259 shorter events, 75.9 us)
Async XLA Ops:
  18.1 25.1 %all-to-all-start.1 = ((f32[1,8,3,128,128]{4,3,2,0,1:T(8,128)}), f32[1,8,3,128,128]{4,3,2,0,1:T(8,128)S(1)}, u32[]{:S(2)}, u32[]{:S(2)}) async-start(f32[1,8,3,128,128]{4,3,2,0,1:T(8,128)} %bitcast.603), calls=%async_computation.1 | async-start | bytes 3145728 | tf_op jit(solution)/shard_map/all_to_all | solution.py:35
  21.7 85.7 %all-gather.41.cloned.1.call-start = ((), (), s32[]{:S(2)}) async-start(), calls=%async_computation.10 | async-start | bytes 1114112 | tf_op jit(solution)/shard_map/all_gather | solution.py:14
  63.8 99.1 %all-gather.25.cloned.1.call-start = ((), (), s32[]{:S(2)}) async-start(), calls=%async_computation.2 | async-start | bytes 1114112 | tf_op jit(solution)/shard_map/all_gather | solution.py:73
  120.7 100.8 %all-gather.43.cloned.1.call-start = ((), (), s32[]{:S(2)}) async-start(), calls=%async_computation.11 | async-start | bytes 1114112 | tf_op jit(solution)/shard_map/all_gather | solution.py:14
  179.2 97.8 %all-gather.27.cloned.1.call-start = ((), (), s32[]{:S(2)}) async-start(), calls=%async_computation.3 | async-start | bytes 1114112 | tf_op jit(solution)/shard_map/all_gather | solution.py:73
  234.8 100.7 %all-gather.45.cloned.1.call-start = ((), (), s32[]{:S(2)}) async-start(), calls=%async_computation.12 | async-start | bytes 1114112 | tf_op jit(solution)/shard_map/all_gather | solution.py:14
  293.2 97.9 %all-gather.29.cloned.1.call-start = ((), (), s32[]{:S(2)}) async-start(), calls=%async_computation.4 | async-start | bytes 1114112 | tf_op jit(solution)/shard_map/all_gather | solution.py:73
  347.9 1.3 copy-start.12
  348.8 100.9 %all-gather.47.cloned.1.call-start = ((), (), s32[]{:S(2)}) async-start(), calls=%async_computation.13 | async-start | bytes 1114112 | tf_op jit(solution)/shard_map/all_gather | solution.py:14
  407.5 98.7 %all-gather.31.cloned.1.call-start = ((), (), s32[]{:S(2)}) async-start(), calls=%async_computation.5 | async-start | bytes 1114112 | tf_op jit(solution)/shard_map/all_gather | solution.py:73
  462.3 1.3 copy-start.14
  463.3 101.5 %all-gather.49.cloned.1.call-start = ((), (), s32[]{:S(2)}) async-start(), calls=%async_computation.14 | async-start | bytes 1114112 | tf_op jit(solution)/shard_map/all_gather | solution.py:14
  463.6 42.6 %copy-start.10 = (f32[1,128,128]{1,2,0:T(8,128)S(1)}, f32[1,128,128]{1,2,0:T(8,128)}, u32[]{:S(2)}) copy-start(f32[1,128,128]{1,2,0:T(8,128)} %get-tuple-element.376) | copy-start | bytes 196612
  522.5 98.7 %all-gather.33.cloned.1.call-start = ((), (), s32[]{:S(2)}) async-start(), calls=%async_computation.6 | async-start | bytes 1114112 | tf_op jit(solution)/shard_map/all_gather | solution.py:73
  577.3 1.3 copy-start.16
  578.3 101.4 %all-gather.51.cloned.1.call-start = ((), (), s32[]{:S(2)}) async-start(), calls=%async_computation.15 | async-start | bytes 1114112 | tf_op jit(solution)/shard_map/all_gather | solution.py:14
  637.5 98.7 %all-gather.35.cloned.1.call-start = ((), (), s32[]{:S(2)}) async-start(), calls=%async_computation.7 | async-start | bytes 1114112 | tf_op jit(solution)/shard_map/all_gather | solution.py:73
  692.3 45.7 %copy-start.18 = (f32[1,128,128]{1,2,0:T(8,128)}, f32[1,128,128]{1,2,0:T(8,128)S(1)}, u32[]{:S(2)}) copy-start(f32[1,128,128]{1,2,0:T(8,128)S(1)} %custom-call.57) | copy-start | bytes 196612
  693.3 101.4 %all-gather.53.cloned.1.call-start = ((), (), s32[]{:S(2)}) async-start(), calls=%async_computation.16 | async-start | bytes 1114112 | tf_op jit(solution)/shard_map/all_gather | solution.py:14
  738.4 74.5 %copy-start.11 = (f32[1,64,2048]{2,1,0:T(8,128)S(1)}, f32[1,64,2048]{2,1,0:T(8,128)}, u32[]{:S(2)}) copy-start(f32[1,64,2048]{2,1,0:T(8,128)} %param.78) | copy-start | bytes 1572868
  750.2 63.5 %copy-start = (f32[1,2048,128]{2,1,0:T(8,128)S(1)}, f32[1,2048,128]{2,1,0:T(8,128)}, u32[]{:S(2)}) copy-start(f32[1,2048,128]{2,1,0:T(8,128)} %all-gather.25.cloned.1.call-done) | copy-start | bytes 3145732
  752.4 103.1 %all-gather.37.cloned.1.call-start = ((), (), s32[]{:S(2)}) async-start(), calls=%async_computation.8 | async-start | bytes 1114112 | tf_op jit(solution)/shard_map/all_gather | solution.py:73
  797.3 18.4 %copy-start.1 = (f32[1,2048,128]{2,1,0:T(8,128)S(1)}, f32[1,2048,128]{2,1,0:T(8,128)}, u32[]{:S(2)}) copy-start(f32[1,2048,128]{2,1,0:T(8,128)} %all-gather.27.cloned.1.call-done) | copy-start | bytes 3145732
  812.6 101.8 %all-gather.55.cloned.1.call-start = ((), (), s32[]{:S(2)}) async-start(), calls=%async_computation.17 | async-start | bytes 1114112 | tf_op jit(solution)/shard_map/all_gather | solution.py:14
  816.8 38.6 %copy-start.9 = (f32[1,128,128]{1,2,0:T(8,128)S(1)}, f32[1,128,128]{1,2,0:T(8,128)}, u32[]{:S(2)}) copy-start(f32[1,128,128]{1,2,0:T(8,128)} %get-tuple-element.382) | copy-start | bytes 196612
  817.1 55.3 %copy-start.13 = (f32[1,128,128]{1,2,0:T(8,128)S(1)}, f32[1,128,128]{1,2,0:T(8,128)}, u32[]{:S(2)}) copy-start(f32[1,128,128]{1,2,0:T(8,128)} %copy-done.12) | copy-start | bytes 196612
  817.1 56.1 %copy-start.2 = (f32[1,2048,128]{2,1,0:T(8,128)S(1)}, f32[1,2048,128]{2,1,0:T(8,128)}, u32[]{:S(2)}) copy-start(f32[1,2048,128]{2,1,0:T(8,128)} %all-gather.29.cloned.1.call-done) | copy-start | bytes 3145732
  857.7 16.6 %copy-start.15 = (f32[1,128,128]{1,2,0:T(8,128)S(1)}, f32[1,128,128]{1,2,0:T(8,128)}, u32[]{:S(2)}) copy-start(f32[1,128,128]{1,2,0:T(8,128)} %copy-done.14) | copy-start | bytes 196612
  857.8 17.4 %copy-start.3 = (f32[1,2048,128]{1,2,0:T(8,128)S(1)}, f32[1,2048,128]{1,2,0:T(8,128)}, u32[]{:S(2)}) copy-start(f32[1,2048,128]{1,2,0:T(8,128)} %all-gather.31.cloned.1.call-done) | copy-start | bytes 3145732
  872.1 98.1 %all-gather.39.cloned.1.call-start = ((), (), s32[]{:S(2)}) async-start(), calls=%async_computation.9 | async-start | bytes 1114112 | tf_op jit(solution)/shard_map/all_gather | solution.py:73
  873.2 2.5 copy-start.17
  873.2 3.3 copy-start.4
  876.5 51.4 %copy-start.19 = (f32[1,128,128]{1,2,0:T(8,128)S(1)}, f32[1,128,128]{1,2,0:T(8,128)}, u32[]{:S(2)}) copy-start(f32[1,128,128]{1,2,0:T(8,128)} %copy-done.18) | copy-start | bytes 196612
  877.1 51.6 %copy-start.5 = (f32[1,2048,128]{1,2,0:T(8,128)S(1)}, f32[1,2048,128]{1,2,0:T(8,128)}, u32[]{:S(2)}) copy-start(f32[1,2048,128]{1,2,0:T(8,128)} %all-gather.35.cloned.1.call-done) | copy-start | bytes 3145732
  915.7 13.5 %copy-start.20 = (f32[1,128,128]{1,2,0:T(8,128)S(1)}, f32[1,128,128]{1,2,0:T(8,128)}, u32[]{:S(2)}) copy-start(f32[1,128,128]{1,2,0:T(8,128)} %custom-call.59) | copy-start | bytes 196612
  915.7 14.3 %copy-start.6 = (f32[1,2048,128]{1,2,0:T(8,128)S(1)}, f32[1,2048,128]{1,2,0:T(8,128)}, u32[]{:S(2)}) copy-start(f32[1,2048,128]{1,2,0:T(8,128)} %all-gather.37.cloned.1.call-done) | copy-start | bytes 3145732
  928.7 41.5 %copy-start.8 = (f32[1,128,128]{2,1,0:T(8,128)S(1)}, f32[1,128,128]{2,1,0:T(8,128)}, u32[]{:S(2)}) copy-start(f32[1,128,128]{2,1,0:T(8,128)} %get-tuple-element.384) | copy-start | bytes 196612
  974.4 1.3 copy-start.7
  974.4 1.6 copy-start.21
  976.7 0.8 copy-start.22
Sparse Core Ops, SparseCore 0:
  63.9 43.3 all-gather.40
  120.8 42.0 all-gather.24
  179.3 42.0 all-gather.42
  234.9 42.0 all-gather.26
  293.4 42.0 all-gather.44
  349.0 42.0 all-gather.28
  407.6 42.1 all-gather.46
  463.4 42.7 all-gather.30
  522.6 42.1 all-gather.48
  578.5 42.7 all-gather.32
  637.6 42.1 all-gather.50
  693.4 42.7 all-gather.34
  752.5 42.1 all-gather.52
  812.7 42.7 all-gather.36
  872.3 42.1 all-gather.54
  928.0 42.1 all-gather.38
